TPU v7x, 128 devices: a whole 4x4x4 slice. The times are simulated.
128 devices in a mesh: prow: 8 (over y, core), pcol: 16 (over x, z).
Axes of the slice: x: 4, y: 4, z: 4, core: 2. Of those that a mesh axis runs over, the one named last changes fastest.
Arguments:
- cross_cov: float32 [2, 512, 16384], P(None, 'prow', 'pcol'), may hold values from -6 to 6
- prev_rows: bfloat16 [2, 512, 32768], P(None, 'pcol', 'prow'), may hold values from -0.046875 to 0.046875
- prev_solved: bfloat16 [32768, 16384], P('prow', 'pcol'), may hold values from -6 to 6
- sub_block: float32 [512, 512], replicated, may hold values from -0.25 to 0.25
- inv_first: float32 [512, 512], replicated, as said below
- inv_second: float32 [512, 512], replicated, as said below
Outputs:
- solved: float32 [2, 512, 16384], P(None, 'prow', 'pcol')
Inputs may be any that keep to these rules, and one draw needn't show every extreme that they name: inv_first is lower triangular with a positive diagonal. inv_second is lower triangular with a positive diagonal.
All inputs are finite; a program needn't handle non-finite values.
Results may differ from a plain program's by a relative error of at most 0.0003.
Values may be sent and summed in bfloat16 or wider, within the bound.
A program may use at most 64 MiB of HBM per device.

v0:
```python
import jax
import jax.numpy as jnp
from jax import lax
from jax.sharding import PartitionSpec as P


def mult(left, right):
    return jnp.dot(left, right, preferred_element_type=jnp.float32, precision=lax.Precision.HIGH)


def local(cross_cov, prev_rows, prev_solved, sub_block, inv_first, inv_second):
    rows = cross_cov.shape[1]
    terms = jnp.einsum(
        "kra,ac->krc",
        lax.all_gather(prev_rows, "pcol", axis=1, tiled=True),
        prev_solved,
        preferred_element_type=jnp.float32,
    )
    offset = lax.axis_index("prow") * rows
    rhs = lax.dynamic_update_slice_in_dim(
        -terms, lax.dynamic_slice_in_dim(-terms, offset, rows, 1) + cross_cov, offset, 1
    )
    first = mult(inv_first, rhs[0])
    second = mult(inv_second, rhs[1] - mult(sub_block, first))
    both = jnp.concatenate([first, second]).reshape((2,) + first.shape)
    return lax.psum_scatter(both, "prow", scatter_dimension=1, tiled=True)


def solution(mesh):
    return jax.shard_map(
        local,
        mesh=mesh,
        in_specs=(
            P(None, "prow", "pcol"),
            P(None, "pcol", "prow"),
            P("prow", "pcol"),
            P(),
            P(),
            P(),
        ),
        out_specs=P(None, "prow", "pcol"),
        check_vma=False,
    )
```

profile of v0, /device:TPU:0, one launch (start us, length us, event | category | flops | bytes accessed | tf_op | source)
XLA Modules:
  0.0 148.7 jit_solution(808641312518555056)
XLA Ops:
  6.5 0.0 copy-start
  6.5 0.0 all-gather.2.cloned.1.call-start
  6.5 0.7 all-gather.2.cloned.1.call-update
  7.3 0.0 reduce-scatter.2.cloned.1.call-start
  7.3 0.0 copy-start.3
  7.3 75.6 %all-gather.2.cloned.1.call-done = bf16[2,512,4096]{2,1,0:T(8,128)(2,1)} async-done(((bf16[2,32,4096]{2,1,0:T(8,128)(2,1)}), bf16[2,512,4096]{2,1,0:T(8,128)(2,1)}) %all-gather.2.cloned.1.call-update) | async-done | bytes 8388624 | tf_op jit(solution)/shard_map/all_gather | solution.py:15
  82.9 13.1 %fusion.2 = f32[2,512,1024]{2,1,0:T(8,128)S(1)} fusion(bf16[2,512,4096]{2,1,0:T(8,128)(2,1)} %all-gather.2.cloned.1.call-done, bf16[4096,1024]{1,0:T(8,128)(2,1)} %param.8), kind=kOutput, calls=%fused_computation.3 | convolution fusion | flops 8590983168 | bytes 20971520 | tf_op jit(solution)/shard_map/kra,ac->krc/dot_general | solution.py:13
  96.0 0.0 copy-done.3
  96.0 0.0 copy-start.1
  96.0 0.1 add_dynamic-update-slice_fusion
  96.2 0.0 copy-done
  96.2 0.0 copy-start.2
  96.2 1.9 %fusion.8 = f32[1024,512]{0,1:T(8,128)S(1)} fusion(f32[512,512]{1,0:T(8,128)S(1)} %copy-done, f32[2,512,1024]{2,1,0:T(8,128)S(1)} %add_dynamic-update-slice_fusion), kind=kOutput, calls=%fused_computation.8 | convolution fusion | flops 1610612736 | bytes 5242880 | tf_op jit(solution)/shard_map/dot_general | solution.py:8
  98.0 0.0 copy-done.1
  98.1 1.9 %fusion.13 = f32[1024,512]{0,1:T(8,128)S(1)} fusion(f32[1024,512]{0,1:T(8,128)S(1)} %fusion.8, f32[512,512]{1,0:T(8,128)S(1)} %copy-done.1), kind=kOutput, calls=%fused_computation.12 | convolution fusion | flops 1610612736 | bytes 5242880 | tf_op jit(solution)/shard_map/dot_general | solution.py:8
  100.0 0.0 copy-done.2
  100.0 1.9 %fusion.10 = f32[512,1024]{1,0:T(8,128)S(1)} fusion(f32[512,512]{1,0:T(8,128)S(1)} %copy-done.2, f32[2,512,1024]{2,1,0:T(8,128)S(1)} %add_dynamic-update-slice_fusion, f32[1024,512]{0,1:T(8,128)S(1)} %fusion.13), kind=kOutput, calls=%fused_computation.10 | convolution fusion | flops 1611137024 | bytes 7340032 | tf_op jit(solution)/shard_map/dot_general | solution.py:8
  101.9 2.5 %pad_maximum_fusion = f32[1024,1024]{1,0:T(8,128)} fusion(f32[512,1024]{1,0:T(8,128)S(1)} %fusion.10, f32[512,1024]{1,0:T(8,128)S(1)} %bitcast.31), kind=kLoop, calls=%fused_computation.2 | loop fusion | flops 1048576 | bytes 8388608 | tf_op jit(solution)/shard_map/concatenate | solution.py:25
  104.3 0.0 reduce-scatter.2.cloned.1.call-update
  104.4 37.5 %reduce-scatter.2.cloned.1.call-done = f32[2,64,1024]{2,1,0:T(8,128)} async-done(((f32[2,512,1024]{2,1,0:T(8,128)}), f32[2,64,1024]{2,1,0:T(8,128)}) %reduce-scatter.2.cloned.1.call-update) | async-done | bytes 524304 | tf_op jit(solution)/shard_map/reduce_scatter | solution.py:26
Async XLA Ops:
  6.5 89.6 %copy-start = (f32[512,512]{1,0:T(8,128)S(1)}, f32[512,512]{1,0:T(8,128)}, u32[]{:S(2)}) copy-start(f32[512,512]{1,0:T(8,128)} %param.10) | copy-start | bytes 3145732
  6.5 76.4 %all-gather.2.cloned.1.call-start = ((), (), s32[]{:S(2)}) async-start(), calls=%async_computation.1 | async-start | bytes 8912896 | tf_op jit(solution)/shard_map/all_gather | solution.py:15
  7.3 134.6 %reduce-scatter.2.cloned.1.call-start = ((), (), s32[]{:S(2)}) async-start(), calls=%async_computation.2 | async-start | bytes 4718592 | tf_op jit(solution)/shard_map/reduce_scatter | solution.py:26
  7.3 88.7 %copy-start.3 = (f32[2,64,1024]{2,1,0:T(8,128)S(1)}, f32[2,64,1024]{2,1,0:T(8,128)}, u32[]{:S(2)}) copy-start(f32[2,64,1024]{2,1,0:T(8,128)} %param.6) | copy-start | bytes 1572868
  96.0 2.0 %copy-start.1 = (f32[512,512]{1,0:T(8,128)S(1)}, f32[512,512]{1,0:T(8,128)}, u32[]{:S(2)}) copy-start(f32[512,512]{1,0:T(8,128)} %param.9) | copy-start | bytes 3145732
  96.2 3.8 %copy-start.2 = (f32[512,512]{1,0:T(8,128)S(1)}, f32[512,512]{1,0:T(8,128)}, u32[]{:S(2)}) copy-start(f32[512,512]{1,0:T(8,128)} %param.11) | copy-start | bytes 3145732
Sparse Core Ops, SparseCore 0:
  9.6 73.3 all-gather.1
  104.5 37.3 reduce-scatter.1
where the time goes:
time: 149 us
  waiting for transfers between devices  114 us (77%)
  matrix products  18.7 us (13%)
  between operations  13.5 us (9%)
  other arithmetic  2.58 us (2%)
    all_gather x1, waiting for transfers between devices, local(): lax.all_gather(prev_rows, 'pcol', axis=1, tiled=True)  75.6 us
    reduce_scatter x1, waiting for transfers between devices, local(): return lax.psum_scatter(both, 'prow', scatter_dimension=1, tiled=True)  37.5 us
    dot_general x1, matrix products, local(): jnp.einsum('kra,ac->krc', lax.all_gather(prev_rows, 'pcol', axis=1, tiled...  13.1 us
    dot_general x3, matrix products, mult(): jnp.dot(left, right, preferred_element_type=jnp.float32, precision=lax.Pr...  5.64 us
  transfers between devices with their start and end apart: 2, of which 2 were waited for; matrix products, arithmetic and copies ran while one was open for 0% of the time, Pallas kernels for 0%

commit v1 on v0

--- a/solution.py
+++ b/solution.py
@@ -12,7 +12,9 @@
     rows = cross_cov.shape[1]
     terms = jnp.einsum(
         "kra,ac->krc",
-        lax.all_gather(prev_rows, "pcol", axis=1, tiled=True),
+        jnp.concatenate(
+            lax.all_to_all(jnp.stack([prev_rows] * lax.axis_size("pcol")), "pcol", 0, 0), axis=1
+        ),
         prev_solved,
         preferred_element_type=jnp.float32,
     )

time: 149 us -> 245 us (1.64)
  waiting for transfers between devices: 114 us -> 188 us
  local copies, waits for them, and re-layouts: 0.02 us -> 13.2 us
  starting transfers between devices: 0.04 us -> 8.05 us
    all_to_all x0 -> x1, waiting for transfers between devices: none -> 148 us  [local(): lax.all_to_all(jnp.stack([prev_rows] * lax.axis_size('pcol')), 'pcol', 0, 0)]
    all_gather x1 -> x0, waiting for transfers between devices: 75.6 us -> none  [local(): lax.all_gather(prev_rows, 'pcol', axis=1, tiled=True)]
    all_to_all x0 -> x1, starting transfers between devices: none -> 8.01 us  [local(): lax.all_to_all(jnp.stack([prev_rows] * lax.axis_size('pcol')), 'pcol', 0, 0)]
    reshape x0 -> x1, local copies, waits for them, and re-layouts: none -> 7.72 us  [local(): jnp.concatenate(lax.all_to_all(jnp.stack([prev_rows] * lax.axis_size('pco...]
    another operation x0 -> x1, local copies, waits for them, and re-layouts: none -> 5.43 us  [local(): jnp.stack([prev_rows] * lax.axis_size('pcol'))]
    reduce_scatter x1, waiting for transfers between devices: 37.5 us -> 40.8 us  [local(): return lax.psum_scatter(both, 'prow', scatter_dimension=1, tiled=True)]
where the time goes in v1:
time: 245 us
  waiting for transfers between devices  188 us (77%)
  matrix products  18.8 us (8%)
  between operations  13.5 us (6%)
  local copies, waits for them, and re-layouts  13.2 us (5%)
  starting transfers between devices  8.05 us (3%)
  other arithmetic  2.57 us (1%)
    all_to_all x1, waiting for transfers between devices, local(): lax.all_to_all(jnp.stack([prev_rows] * lax.axis_size('pcol')), 'pcol', 0, 0)  148 us
    reduce_scatter x1, waiting for transfers between devices, local(): return lax.psum_scatter(both, 'prow', scatter_dimension=1, tiled=True)  40.8 us
    dot_general x1, matrix products, local(): jnp.einsum('kra,ac->krc', jnp.concatenate(lax.all_to_all(jnp.stack([prev_...  13.1 us
    all_to_all x1, starting transfers between devices, local(): lax.all_to_all(jnp.stack([prev_rows] * lax.axis_size('pcol')), 'pcol', 0, 0)  8.01 us
    reshape x1, local copies, waits for them, and re-layouts, local(): jnp.concatenate(lax.all_to_all(jnp.stack([prev_rows] * lax.axis_size('pco...  7.72 us
    dot_general x3, matrix products, mult(): jnp.dot(left, right, preferred_element_type=jnp.float32, precision=lax.Pr...  5.64 us
    another operation x1, local copies, waits for them, and re-layouts, local(): jnp.stack([prev_rows] * lax.axis_size('pcol'))  5.43 us
  transfers between devices with their start and end apart: 2, of which 2 were waited for; matrix products, arithmetic and copies ran while one was open for 0% of the time, Pallas kernels for 0%

profile of v1, /device:TPU:0, one launch (start us, length us, event | category | flops | bytes accessed | tf_op | source)
XLA Modules:
  0.0 244.5 jit_solution(6928259550333994259)
XLA Ops:
  6.5 0.0 copy-start
  6.5 5.4 %stack.2 = bf16[16,2,32,4096]{3,2,1,0:T(8,128)(2,1)} broadcast(bf16[2,32,4096]{2,1,0:T(8,128)(2,1)} %param.7), dimensions={1,2,3} | broadcast | bytes 8912896 | tf_op jit(solution)/shard_map/stack | solution.py:16
  12.0 8.0 %all-to-all-start = ((bf16[16,2,32,4096]{3,2,1,0:T(8,128)(2,1)}), bf16[16,2,32,4096]{3,2,1,0:T(8,128)(2,1)}, u32[]{:S(2)}, u32[]{:S(2)}) async-start(bf16[16,2,32,4096]{3,2,1,0:T(8,128)(2,1)} %stack.2), calls=%async_computation | async-start | bytes 16777216 | tf_op jit(solution)/shard_map/all_to_all | solution.py:16
  20.0 0.0 reduce-scatter.2.cloned.1.call-start
  20.0 147.6 %all-to-all-done = bf16[16,2,32,4096]{3,2,1,0:T(8,128)(2,1)} async-done(((bf16[16,2,32,4096]{3,2,1,0:T(8,128)(2,1)}), bf16[16,2,32,4096]{3,2,1,0:T(8,128)(2,1)}, u32[]{:S(2)}, u32[]{:S(2)}) %all-to-all-start) | async-done | bytes 8388640 | tf_op jit(solution)/shard_map/all_to_all | solution.py:16
  167.7 7.7 %copy.7 = bf16[2,16,32,4096]{3,2,1,0:T(8,128)(2,1)} copy(bf16[2,16,32,4096]{3,2,0,1:T(8,128)(2,1)} %bitcast) | data formatting | bytes 16777216 | tf_op jit(solution)/shard_map/reshape | solution.py:15
  175.4 0.0 copy-start.3
  175.4 13.1 %fusion.2 = f32[2,512,1024]{2,1,0:T(8,128)S(1)} fusion(bf16[2,512,4096]{2,1,0:T(8,128)(2,1)} %bitcast.35, bf16[4096,1024]{1,0:T(8,128)(2,1)} %param.8), kind=kOutput, calls=%fused_computation.3 | convolution fusion | flops 8590983168 | bytes 20971520 | tf_op jit(solution)/shard_map/kra,ac->krc/dot_general | solution.py:13
  188.5 0.0 copy-done.3
  188.5 0.0 copy-start.1
  188.5 0.1 add_dynamic-update-slice_fusion
  188.6 0.0 copy-done
  188.7 0.0 copy-start.2
  188.7 1.9 fusion.8
  190.5 0.0 copy-done.1
  190.5 1.9 fusion.13
  192.4 0.0 copy-done.2
  192.4 1.9 fusion.10
  194.3 2.5 %pad_maximum_fusion = f32[1024,1024]{1,0:T(8,128)} fusion(f32[512,1024]{1,0:T(8,128)S(1)} %fusion.10, f32[512,1024]{1,0:T(8,128)S(1)} %bitcast.33), kind=kLoop, calls=%fused_computation.2 | loop fusion | flops 1048576 | bytes 8388608 | tf_op jit(solution)/shard_map/concatenate | solution.py:27
  196.8 0.0 reduce-scatter.2.cloned.1.call-update
  196.8 40.8 %reduce-scatter.2.cloned.1.call-done = f32[2,64,1024]{2,1,0:T(8,128)} async-done(((f32[2,512,1024]{2,1,0:T(8,128)}), f32[2,64,1024]{2,1,0:T(8,128)}) %reduce-scatter.2.cloned.1.call-update) | async-done | bytes 524304 | tf_op jit(solution)/shard_map/reduce_scatter | solution.py:28
Async XLA Ops:
  6.5 182.1 %copy-start = (f32[512,512]{1,0:T(8,128)S(1)}, f32[512,512]{1,0:T(8,128)}, u32[]{:S(2)}) copy-start(f32[512,512]{1,0:T(8,128)} %param.10) | copy-start | bytes 3145732
  12.0 155.7 %all-to-all-start = ((bf16[16,2,32,4096]{3,2,1,0:T(8,128)(2,1)}), bf16[16,2,32,4096]{3,2,1,0:T(8,128)(2,1)}, u32[]{:S(2)}, u32[]{:S(2)}) async-start(bf16[16,2,32,4096]{3,2,1,0:T(8,128)(2,1)} %stack.2), calls=%async_computation | async-start | bytes 16777216 | tf_op jit(solution)/shard_map/all_to_all | solution.py:16
  20.0 217.7 %reduce-scatter.2.cloned.1.call-start = ((), (), s32[]{:S(2)}) async-start(), calls=%async_computation.2 | async-start | bytes 4718592 | tf_op jit(solution)/shard_map/reduce_scatter | solution.py:28
  175.4 13.2 %copy-start.3 = (f32[2,64,1024]{2,1,0:T(8,128)S(1)}, f32[2,64,1024]{2,1,0:T(8,128)}, u32[]{:S(2)}) copy-start(f32[2,64,1024]{2,1,0:T(8,128)} %param.6) | copy-start | bytes 1572868
  188.5 2.0 copy-start.1
  188.7 3.8 %copy-start.2 = (f32[512,512]{1,0:T(8,128)S(1)}, f32[512,512]{1,0:T(8,128)}, u32[]{:S(2)}) copy-start(f32[512,512]{1,0:T(8,128)} %param.11) | copy-start | bytes 3145732
Sparse Core Ops, SparseCore 0:
  197.0 40.6 reduce-scatter.1
